TPU v7x, 32 devices: a whole 2x2x4 slice. The times are simulated.
32 devices in a mesh: clips: 2 (over y), space: 4 (over z), tm: 2 (over x), chan: 2 (over core).
Axes of the slice: x: 2, y: 2, z: 4, core: 2. Of those that a mesh axis runs over, the one named last changes fastest.
Arguments:
- frames_in: bfloat16 [4, 16, 160, 384], P(('clips', 'tm'), 'space', None, 'chan'), parts along dimension 0, may hold values from -6 to 6
- cache: bfloat16 [4, 16, 160, 384], P('clips', 'space'), parts along dimension 0, may hold values from -6 to 6
- gain_one: bfloat16 [384], replicated, may hold values from 0.099609375 to 1.8984375
- gain_two: bfloat16 [384], replicated, may hold values from 0.099609375 to 1.8984375
- w_query: bfloat16 [384, 384], replicated, may hold values from -10 to 10
- w_key: bfloat16 [384, 384], replicated, may hold values from -10 to 10
- w_value: bfloat16 [384, 384], replicated, may hold values from -0.3125 to 0.3125
- w_out: bfloat16 [384, 384], replicated, may hold values from -0.3125 to 0.3125
- conv_weight: bfloat16 [3, 3, 3, 384, 384], P(None, None, None, None, 'chan'), may hold values from -0.0625 to 0.0625
Outputs:
- decoded: bfloat16 [4, 16, 160, 384], P(('clips', 'tm'), 'space', None, 'chan'), parts along dimension 0
There are 2 independent parts, one for each index of `clips`. A program takes and returns all parts, laid end to end along the dimension named above; an argument that names none is the same for every part. Nothing has to cross between parts.
All inputs are finite; a program needn't handle non-finite values.
Results may differ from a plain program's by a relative error of at most 0.0062.
Values may be sent and summed in bfloat16 or wider, within the bound.
A program may use at most 128 MiB of HBM per device.

v0:
```python
import jax
import jax.numpy as jnp
from jax import lax
from jax.sharding import PartitionSpec as P


def from_behind(array, axis, by):
    devices = lax.axis_size(axis)
    pairs = [(i, i + by) for i in range(devices) if 0 <= i + by < devices]
    return lax.ppermute(array, axis, pairs)


def padded_2(cells, sides, width):
    for axis, dim in sides:
        count = lax.axis_size(axis)
        ends = count - 1
        head = lax.slice_in_dim(cells, 0, width, axis=dim)
        tail = lax.slice_in_dim(cells, cells.shape[dim] - width, cells.shape[dim], axis=dim)
        cells = jnp.concatenate(
            [
                lax.ppermute(tail, axis, [(i, (i + 1) % count) for i in range(ends)]),
                cells,
                lax.ppermute(head, axis, [((i + 1) % count, i) for i in range(ends)]),
            ],
            axis=dim,
        )
    return cells


def rms_scaled(values, gain):
    wide = values.astype(jnp.float32)
    factor = lax.rsqrt(jnp.mean(wide * wide, axis=-1, keepdims=True) + 1e-06)
    return wide * factor * gain.astype(jnp.float32)


def body(frames_in, cache, gain_one, gain_two, w_query, w_key, w_value, w_out, conv_weight):
    mine = lax.axis_index("chan")
    own = lax.all_to_all(frames_in, "chan", split_axis=1, concat_axis=3, tiled=True)
    half_rows, cells, width = (own.shape[1], own.shape[2], own.shape[3])
    tokens = own.reshape(half_rows * cells, width)
    normed = rms_scaled(tokens, gain_one).astype(jnp.bfloat16)
    query = jnp.dot(normed, w_query, preferred_element_type=jnp.float32).astype(jnp.bfloat16)
    scale = width ** (-0.5)
    count = tokens.shape[0]
    piece = lax.all_gather(normed, ("space", "chan"), axis=0, tiled=True)
    keys = jnp.dot(piece, w_key, preferred_element_type=jnp.float32).astype(jnp.bfloat16)
    values = jnp.dot(piece, w_value, preferred_element_type=jnp.float32).astype(jnp.bfloat16)
    top = jnp.full((count, 1), -1e30, jnp.float32)
    scores = jnp.einsum("qc,kc->qk", query, keys, preferred_element_type=jnp.float32) * scale
    new_top = jnp.maximum(top, jnp.max(scores, axis=-1, keepdims=True))
    weights = jnp.exp(scores - new_top)
    total = jnp.sum(weights, axis=-1, keepdims=True)
    accum = jnp.dot(weights.astype(jnp.bfloat16), values, preferred_element_type=jnp.float32)
    top, total, accum = (new_top, total, accum)
    attended = (accum / total).astype(jnp.bfloat16)
    joined = tokens.astype(jnp.float32) + jnp.dot(
        attended, w_out, preferred_element_type=jnp.float32
    )
    joined = joined.astype(jnp.bfloat16).reshape(1, half_rows, cells, width)
    whole = lax.all_gather(joined, "chan", axis=1, tiled=True)
    act = jax.nn.silu(rms_scaled(whole, gain_two)).astype(jnp.bfloat16)
    moment = lax.axis_index("tm")
    first = from_behind(act, "tm", 1)
    second = from_behind(act, "tm", 2)
    prev_one = jnp.where(moment == 0, cache[1:2], first)
    prev_two = jnp.where(moment == 0, cache[0:1], jnp.where(moment == 1, cache[1:2], second))
    stacked = jnp.concatenate([prev_two, prev_one, act], axis=0)
    rimmed = padded_2(stacked, (("space", 1),), 1)
    padded = jnp.pad(rimmed, ((0, 0), (0, 0), (1, 1), (0, 0)))
    conv = lax.conv_general_dilated(
        padded[None],
        conv_weight,
        (1, 1, 1),
        "VALID",
        dimension_numbers=("NDHWC", "DHWIO", "NDHWC"),
        preferred_element_type=jnp.float32,
    )[0]
    share = conv_weight.shape[4]
    own_joined = lax.dynamic_slice_in_dim(whole, mine * share, share, 3)
    return (own_joined.astype(jnp.float32) + conv).astype(jnp.bfloat16)


def solution(mesh):
    return jax.shard_map(
        body,
        mesh=mesh,
        in_specs=(
            P(("clips", "tm"), "space", None, "chan"),
            P("clips", "space", None, None),
            P(),
            P(),
            P(),
            P(),
            P(),
            P(),
            P(None, None, None, None, "chan"),
        ),
        out_specs=P(("clips", "tm"), "space", None, "chan"),
        check_vma=False,
    )
```

profile of v0, /device:TPU:0, one launch (start us, length us, event | category | flops | bytes accessed | tf_op | source)
XLA Modules:
  0.0 116.3 jit_solution(1926624197613109839)
XLA Ops:
  6.5 0.0 copy-start
  6.5 0.0 all-gather.2.cloned.1.call-start
  6.6 5.2 %all_to_all.4 = bf16[1,4,160,192]{3,2,0,1:T(8,128)(2,1)S(1)} all-to-all(bf16[1,4,160,192]{3,2,0,1:T(8,128)(2,1)} %bitcast.55), channel_id=1, replica_groups=mesh['clips'=2,'space'=4,'tm'=2,'chan'=2] {'chan'}, dimensions={1} | all-to-all | bytes 491520 | tf_op jit(solution)/shard_map/all_to_all | solution.py:38
  11.8 0.3 copy.58
  12.1 0.5 reshape.60
  12.6 0.2 multiply_reduce_fusion
  12.9 0.1 rsqrt.20
  13.0 0.0 copy-done.4
  13.0 0.8 multiply_convert_fusion
  13.8 0.0 all-gather.2.cloned.1.call-update
  13.8 0.0 copy-done.5
  13.8 0.0 copy-done.2
  13.8 1.3 %convolution_convert_fusion.2 = bf16[320,384]{1,0:T(8,128)(2,1)S(1)} fusion(bf16[320,384]{1,0:T(8,128)(2,1)} %multiply_convert_fusion, bf16[384,384]{1,0:T(8,128)(2,1)S(1)} %copy-done.2), kind=kOutput, calls=%fused_computation.32 | convolution fusion | flops 94494720 | bytes 786432 | tf_op jit(solution)/shard_map/dot_general | solution.py:42
  15.1 29.6 %all-gather.2.cloned.1.call-done = bf16[2560,384]{1,0:T(8,128)(2,1)} async-done(((bf16[320,384]{1,0:T(8,128)(2,1)}), bf16[2560,384]{1,0:T(8,128)(2,1)}) %all-gather.2.cloned.1.call-update) | async-done | bytes 1966096 | tf_op jit(solution)/shard_map/all_gather | solution.py:45
  44.7 5.4 %fusion.46 = (f32[320]{0:T(512)S(1)}, f32[320,2560]{1,0:T(8,128)}) fusion(bf16[320,384]{1,0:T(8,128)(2,1)S(1)} %convolution_convert_fusion.2, bf16[2560,384]{1,0:T(8,128)(2,1)} %all-gather.2.cloned.1.call-done, bf16[384,384]{1,0:T(8,128)(2,1)S(1)} %copy-done), kind=kOutput, calls=%fused_computation.64 | convolution fusion | flops 1386741504 | bytes 5784832 | tf_op jit(solution)/shard_map/qc,kc->qk/dot_general | solution.py:49
  50.1 2.6 %fusion.2 = f32[320]{0:T(512)S(1)} fusion(f32[320,2560]{1,0:T(8,128)} %get-tuple-element.10, f32[320]{0:T(512)S(1)} %broadcast_maximum_fusion), kind=kLoop, calls=%fused_computation.9 | loop fusion | flops 1638080 | bytes 3279360 | tf_op jit(solution)/shard_map/reduce_sum | solution.py:52
  52.7 0.0 copy-start.3
  52.7 4.8 %fusion.28 = bf16[320,384]{1,0:T(8,128)(2,1)S(1)} fusion(f32[320,2560]{1,0:T(8,128)} %get-tuple-element.10, f32[320]{0:T(512)S(1)} %broadcast_maximum_fusion, bf16[2560,384]{1,0:T(8,128)(2,1)} %all-gather.2.cloned.1.call-done, bf16[384,384]{1,0:T(8,128)(2,1)S(1)} %copy-done.7, f32[320]{0:T(512)S(1)} %fusion.2), kind=kOutput, calls=%fused_computation.35 | convolution fusion | flops 1386987520 | bytes 5786112 | tf_op jit(solution)/shard_map/dot_general | solution.py:53
  57.5 0.0 copy-done.3
  57.5 0.0 copy-start.1
  57.5 0.3 fusion.24
  57.9 2.2 %all_gather.7 = bf16[1,4,160,384]{3,2,0,1:T(8,128)(2,1)S(1)} all-gather(bf16[1,2,160,384]{3,2,0,1:T(8,128)(2,1)S(1)} %bitcast.53), channel_id=1, replica_groups=mesh['clips'=2,'space'=4,'tm'=2,'chan'=2] {'chan'}, dimensions={1}, use_global_device_ids=true | all-gather | bytes 737280 | tf_op jit(solution)/shard_map/all_gather | solution.py:60
  60.0 0.2 fusion.31
  60.3 0.4 fusion.38
  60.6 1.4 %collective-permute-start = (bf16[1,4,160,384]{3,2,0,1:T(8,128)(2,1)S(1)}, bf16[1,4,160,384]{3,2,0,1:T(8,128)(2,1)}, u32[]{:S(2)}, u32[]{:S(2)}) collective-permute-start(bf16[1,4,160,384]{3,2,0,1:T(8,128)(2,1)S(1)} %fusion.38), channel_id=1, source_target_pairs={} | collective-permute-start | bytes 1474568 | tf_op jit(solution)/shard_map/ppermute | solution.py:10
  62.1 4.2 %collective-permute-start.1 = (bf16[1,4,160,384]{3,2,0,1:T(8,128)(2,1)S(1)}, bf16[1,4,160,384]{3,2,0,1:T(8,128)(2,1)}, u32[]{:S(2)}, u32[]{:S(2)}) collective-permute-start(bf16[1,4,160,384]{3,2,0,1:T(8,128)(2,1)S(1)} %fusion.38), channel_id=1, source_target_pairs={{0,2},{1,3},{4,6},{5,7},{8,10},{9,11},{12,14},{13,15},{16,18},{17,... | collective-permute-start | bytes 1474568 | tf_op jit(solution)/shard_map/ppermute | solution.py:10
  66.2 0.0 collective-permute-done
  66.2 10.1 %collective-permute-done.1 = bf16[1,4,160,384]{3,2,0,1:T(8,128)(2,1)} collective-permute-done((bf16[1,4,160,384]{3,2,0,1:T(8,128)(2,1)S(1)}, bf16[1,4,160,384]{3,2,0,1:T(8,128)(2,1)}, u32[]{:S(2)}, u32[]{:S(2)}) %collective-permute-start.1) | collective-permute-done | bytes 491552 | tf_op jit(solution)/shard_map/ppermute | solution.py:10
  76.3 1.1 fusion.41
  77.5 1.0 maximum_bitcast_fusion
  78.4 3.5 %collective-permute-start.2 = (bf16[3,1,160,384]{3,2,1,0:T(8,128)(2,1)}, bf16[3,1,160,384]{3,2,1,0:T(8,128)(2,1)S(1)}, u32[]{:S(2)}, u32[]{:S(2)}) collective-permute-start(bf16[3,1,160,384]{3,2,1,0:T(8,128)(2,1)} %get-tuple-element.5), channel_id=1, source_target_pairs={{0,4},{4,8},{8,12},{1,5},{5,9},{9,13},{2,6},{6,10},{10,14},{3,7},{... | collective-permute-start | bytes 1105928 | tf_op jit(solution)/shard_map/ppermute | solution.py:21
  81.9 1.5 %collective-permute-start.3 = (bf16[3,1,160,384]{3,2,1,0:T(8,128)(2,1)}, bf16[3,1,160,384]{3,2,1,0:T(8,128)(2,1)}, u32[]{:S(2)}, u32[]{:S(2)}) collective-permute-start(bf16[3,1,160,384]{3,2,1,0:T(8,128)(2,1)} %get-tuple-element.6), channel_id=1, source_target_pairs={{4,0},{8,4},{12,8},{5,1},{9,5},{13,9},{6,2},{10,6},{14,10},{7,3},{... | collective-permute-start | bytes 1105928 | tf_op jit(solution)/shard_map/ppermute | solution.py:23
  83.4 0.2 constant_dynamic-slice_fusion
  83.6 6.1 %collective-permute-done.2 = bf16[3,1,160,384]{3,2,1,0:T(8,128)(2,1)S(1)} collective-permute-done((bf16[3,1,160,384]{3,2,1,0:T(8,128)(2,1)}, bf16[3,1,160,384]{3,2,1,0:T(8,128)(2,1)S(1)}, u32[]{:S(2)}, u32[]{:S(2)}) %collective-permute-start.2) | collective-permute-done | bytes 368672 | tf_op jit(solution)/shard_map/ppermute | solution.py:21
  89.7 4.1 %collective-permute-done.3 = bf16[3,1,160,384]{3,2,1,0:T(8,128)(2,1)} collective-permute-done((bf16[3,1,160,384]{3,2,1,0:T(8,128)(2,1)}, bf16[3,1,160,384]{3,2,1,0:T(8,128)(2,1)}, u32[]{:S(2)}, u32[]{:S(2)}) %collective-permute-start.3) | collective-permute-done | bytes 368672 | tf_op jit(solution)/shard_map/ppermute | solution.py:23
  93.8 3.1 %fusion.11 = bf16[3,6,1,162,384]{4,3,0,1,2:T(8,128)(2,1)S(1)} fusion(bf16[3,1,160,384]{3,2,0,1:T(8,128)(2,1)} %bitcast.8, bf16[3,1,160,384]{3,2,0,1:T(8,128)(2,1)S(1)} %bitcast.54, bf16[1,4,160,384]{3,2,0,1:T(8,128)(2,1)S(1)} %fusion.38, bf16[1,4,160,384]{3,2,0,1:T(8,128)(2,1)S(1)} %get-tuple-element.8, bf16[1,4,160,384]{3,2,0,1:T(8,128)(2,1)S(1)} %get-tuple-element.7), kind=kLoop, calls=%fused_computation.18 | loop fusion | flops 20155392 | bytes 4451328 | tf_op jit(solution)/shard_map/broadcast_in_dim | solution.py:71
  96.9 1.6 %pad.5 = bf16[3,6,1,168,384]{4,3,0,1,2:T(8,128)(2,1)} pad(bf16[3,6,1,162,384]{4,3,0,1,2:T(8,128)(2,1)S(1)} %fusion.11, bf16[]{:T(256)} %constant.34.clone.1), padding=0_0x0_0x0_0x0_6x0_0 | pad | bytes 4561922 | tf_op jit(solution)/shard_map/broadcast_in_dim | solution.py:71
  98.5 3.5 %reshape.69 = bf16[3,6,1,8,21,384]{5,4,3,0,1,2:T(8,128)(2,1)S(1)} reshape(bf16[3,6,1,168,384]{4,3,0,1,2:T(8,128)(2,1)} %pad.5) | data formatting | bytes 4644864 | tf_op jit(solution)/shard_map/conv_general_dilated | solution.py:70
  102.0 0.0 copy-start.6
  102.0 0.0 copy-start.8
  102.1 0.3 copy.47
  102.4 0.1 slice.19
  102.4 1.7 %copy-done.6 = bf16[3,3,3,384,192]{3,4,2,1,0:T(8,128)(2,1)S(1)} copy-done((bf16[3,3,3,384,192]{3,4,2,1,0:T(8,128)(2,1)S(1)}, bf16[3,3,3,384,192]{3,4,2,1,0:T(8,128)(2,1)}, u32[]{:S(2)}) %copy-start.6) | copy-done | bytes 3981336
  104.2 0.0 copy-done.8
  104.2 3.9 %fusion.21 = f32[1,4,8,21,192]{4,2,3,1,0:T(8,128)S(1)} fusion(bf16[3,3,3,384,192]{3,4,2,1,0:T(8,128)(2,1)S(1)} %copy-done.6, bf16[3,6,1,7,2,384]{5,3,4,1,0,2:T(8,128)(2,1)S(1)} %slice.19, bf16[3,6,1,8,21,384]{5,3,4,1,0,2:T(8,128)(2,1)S(1)} %copy.47, pred[8,21]{0,1:T(8,128)(4,1)S(1)} %copy-done.8), kind=kOutput, calls=%fused_computation.28 | convolution fusion | flops 2683201536 | bytes 7013544 | tf_op jit(solution)/shard_map/conv_general_dilated | solution.py:70
  108.1 0.3 copy.48
  108.4 0.3 fusion.40
  108.7 0.8 copy.49
  (14 shorter events, 0.1 us)
Async XLA Ops:
  6.5 38.2 %copy-start = (bf16[384,384]{1,0:T(8,128)(2,1)S(1)}, bf16[384,384]{1,0:T(8,128)(2,1)}, u32[]{:S(2)}) copy-start(bf16[384,384]{1,0:T(8,128)(2,1)} %param.14) | copy-start | bytes 884740
  6.5 6.4 %copy-start.4 = (bf16[384]{0:T(512)(128)(2,1)S(1)}, bf16[384]{0:T(512)(128)(2,1)}, u32[]{:S(2)}) copy-start(bf16[384]{0:T(512)(128)(2,1)} %param.11) | copy-start | bytes 2308
  6.5 7.3 %copy-start.5 = (bf16[384]{0:T(512)(128)(2,1)S(1)}, bf16[384]{0:T(512)(128)(2,1)}, u32[]{:S(2)}) copy-start(bf16[384]{0:T(512)(128)(2,1)} %param.12) | copy-start | bytes 2308
  6.5 7.3 %copy-start.2 = (bf16[384,384]{1,0:T(8,128)(2,1)S(1)}, bf16[384,384]{1,0:T(8,128)(2,1)}, u32[]{:S(2)}) copy-start(bf16[384,384]{1,0:T(8,128)(2,1)} %param.13) | copy-start | bytes 884740
  6.5 38.1 %all-gather.2.cloned.1.call-start = ((), (), s32[]{:S(2)}) async-start(), calls=%async_computation.1 | async-start | bytes 2211840 | tf_op jit(solution)/shard_map/all_gather | solution.py:45
  50.1 2.6 %copy-start.7 = (bf16[384,384]{1,0:T(8,128)(2,1)S(1)}, bf16[384,384]{1,0:T(8,128)(2,1)}, u32[]{:S(2)}) copy-start(bf16[384,384]{1,0:T(8,128)(2,1)} %param.15) | copy-start | bytes 884740
  52.7 4.8 %copy-start.3 = (bf16[384,384]{1,0:T(8,128)(2,1)S(1)}, bf16[384,384]{1,0:T(8,128)(2,1)}, u32[]{:S(2)}) copy-start(bf16[384,384]{1,0:T(8,128)(2,1)} %param.16) | copy-start | bytes 884740
  57.5 18.8 %copy-start.1 = (bf16[2,4,160,384]{3,2,1,0:T(8,128)(2,1)S(1)}, bf16[2,4,160,384]{3,2,1,0:T(8,128)(2,1)}, u32[]{:S(2)}) copy-start(bf16[2,4,160,384]{3,2,1,0:T(8,128)(2,1)} %param.10) | copy-start | bytes 2949124
  60.6 5.6 %collective-permute-start = (bf16[1,4,160,384]{3,2,0,1:T(8,128)(2,1)S(1)}, bf16[1,4,160,384]{3,2,0,1:T(8,128)(2,1)}, u32[]{:S(2)}, u32[]{:S(2)}) collective-permute-start(bf16[1,4,160,384]{3,2,0,1:T(8,128)(2,1)S(1)} %fusion.38), channel_id=1, source_target_pairs={} | collective-permute-start | bytes 1474568 | tf_op jit(solution)/shard_map/ppermute | solution.py:10
  62.1 14.2 %collective-permute-start.1 = (bf16[1,4,160,384]{3,2,0,1:T(8,128)(2,1)S(1)}, bf16[1,4,160,384]{3,2,0,1:T(8,128)(2,1)}, u32[]{:S(2)}, u32[]{:S(2)}) collective-permute-start(bf16[1,4,160,384]{3,2,0,1:T(8,128)(2,1)S(1)} %fusion.38), channel_id=1, source_target_pairs={{0,2},{1,3},{4,6},{5,7},{8,10},{9,11},{12,14},{13,15},{16,18},{17,... | collective-permute-start | bytes 1474568 | tf_op jit(solution)/shard_map/ppermute | solution.py:10
  78.4 11.2 %collective-permute-start.2 = (bf16[3,1,160,384]{3,2,1,0:T(8,128)(2,1)}, bf16[3,1,160,384]{3,2,1,0:T(8,128)(2,1)S(1)}, u32[]{:S(2)}, u32[]{:S(2)}) collective-permute-start(bf16[3,1,160,384]{3,2,1,0:T(8,128)(2,1)} %get-tuple-element.5), channel_id=1, source_target_pairs={{0,4},{4,8},{8,12},{1,5},{5,9},{9,13},{2,6},{6,10},{10,14},{3,7},{... | collective-permute-start | bytes 1105928 | tf_op jit(solution)/shard_map/ppermute | solution.py:21
  81.9 11.9 %collective-permute-start.3 = (bf16[3,1,160,384]{3,2,1,0:T(8,128)(2,1)}, bf16[3,1,160,384]{3,2,1,0:T(8,128)(2,1)}, u32[]{:S(2)}, u32[]{:S(2)}) collective-permute-start(bf16[3,1,160,384]{3,2,1,0:T(8,128)(2,1)} %get-tuple-element.6), channel_id=1, source_target_pairs={{4,0},{8,4},{12,8},{5,1},{9,5},{13,9},{6,2},{10,6},{14,10},{7,3},{... | collective-permute-start | bytes 1105928 | tf_op jit(solution)/shard_map/ppermute | solution.py:23
  102.0 2.1 %copy-start.6 = (bf16[3,3,3,384,192]{3,4,2,1,0:T(8,128)(2,1)S(1)}, bf16[3,3,3,384,192]{3,4,2,1,0:T(8,128)(2,1)}, u32[]{:S(2)}) copy-start(bf16[3,3,3,384,192]{3,4,2,1,0:T(8,128)(2,1)} %param.17) | copy-start | bytes 11943940
  102.0 2.1 %copy-start.8 = (pred[8,21]{0,1:T(8,128)(4,1)S(1)}, pred[8,21]{0,1:T(8,128)(4,1)}, u32[]{:S(2)}) copy-start(pred[8,21]{0,1:T(8,128)(4,1)} %constant.42) | copy-start | bytes 508
Sparse Core Ops, SparseCore 0:
  13.9 30.7 all-gather.1
where the time goes:
time: 117 us; the launch traced here: 116 us
  waiting for transfers between devices  49.9 us (43%)
  matrix products  15.7 us (13%)
  between operations  13.6 us (12%)
  starting transfers between devices  10.6 us (9%)
  other arithmetic  9.76 us (8%)
  local copies, waits for them, and re-layouts  9.41 us (8%)
  blocking collectives  7.34 us (6%)
    all_gather x1, waiting for transfers between devices, body(): piece = lax.all_gather(normed, ('space', 'chan'), axis=0, tiled=True)  29.6 us
    ppermute x2, waiting for transfers between devices, from_behind(): return lax.ppermute(array, axis, pairs)  10.1 us
    ppermute x1, waiting for transfers between devices, padded_2(): lax.ppermute(tail, axis, [(i, (i + 1) % count) for i in range(ends)])  6.08 us
    ppermute x2, starting transfers between devices, from_behind(): return lax.ppermute(array, axis, pairs)  5.6 us
    dot_general x1, matrix products, body(): jnp.einsum('qc,kc->qk', query, keys, preferred_element_type=jnp.float32)  5.41 us
    all_to_all x1, blocking collectives, body(): lax.all_to_all(frames_in, 'chan', split_axis=1, concat_axis=3, tiled=True)  5.19 us
    dot_general x1, matrix products, body(): jnp.dot(weights.astype(jnp.bfloat16), values, preferred_element_type=jnp....  4.79 us
    ppermute x1, waiting for transfers between devices, padded_2(): lax.ppermute(head, axis, [((i + 1) % count, i) for i in range(ends)])  4.14 us
  transfers between devices with their start and end apart: 5, of which 4 were waited for; matrix products, arithmetic and copies ran while one was open for 1% of the time, Pallas kernels for 0%

commit v1 on v0

v1 whole, which is shorter than its diff:
```python
import functools
import math

import jax
import jax.numpy as jnp
from jax import lax
from jax.experimental import pallas as pl
from jax.experimental.pallas import tpu as pltpu
from jax.sharding import PartitionSpec as P

F32 = jnp.float32
BF16 = jnp.bfloat16
MESH = pl.DeviceIdType.MESH


def normalized(wide, gain):
    factor = lax.rsqrt(jnp.mean(wide * wide, axis=-1, keepdims=True) + 1e-06)
    return wide * factor * gain.astype(F32)


def kernel(
    Z, N,
    x_hbm, cache_hbm, g1_ref, g2_ref, wq_hbm, wk_hbm, wv_hbm, wo_hbm, cw_hbm,
    out_ref,
    xr, xg, qk, top, total, acc, cb, jt, jo, parts, wq, wk, wv, wo, cw,
    s_loc, s_pair, r_pair, s_right, s_left, s_sib, r_z, r_sib,
    s_cache, r_halo, s_edge, s_rest, r_edge, r_rest, s_tm, r_tm,
):
    z = lax.axis_index("space")
    c = lax.axis_index("chan")
    tm = lax.axis_index("tm")
    o = 1 - c
    R, W, S = out_ref.shape[1:]
    C = 2 * S
    hr = R // 2
    half = hr * W
    T = R * W

    def dev(dz=None, core=None, frame=None):
        return {
            "space": z if dz is None else dz,
            "chan": c if core is None else core,
            "tm": tm if frame is None else frame,
        }

    def send(src, dst, ssem, rsem, to):
        return pltpu.make_async_remote_copy(
            src_ref=src, dst_ref=dst, send_sem=ssem, recv_sem=rsem,
            device_id=to, device_id_type=MESH,
        )

    near = z + 2 * c - 1
    has_near = jnp.logical_and(near >= 0, near < Z)

    barrier = pltpu.get_barrier_semaphore()

    def greet(to):
        pl.semaphore_signal(barrier, inc=1, device_id=to, device_id_type=MESH)

    greet(dev(core=o))
    pl.when(z > 0)(lambda: greet(dev(dz=z - 1)))
    pl.when(z < Z - 1)(lambda: greet(dev(dz=z + 1)))
    pl.when(has_near)(lambda: greet(dev(dz=near, core=o)))
    for hop in (1, 2):
        if N > hop:
            pl.when(tm >= hop)(functools.partial(lambda h: greet(dev(frame=tm - h)), hop))

    x_own = pltpu.make_async_copy(x_hbm.at[0, pl.ds(c * hr, hr)], xr.at[c], s_loc.at[0])
    x_own.start()
    weights = [
        pltpu.make_async_copy(a, b, s_loc.at[1 + i])
        for i, (a, b) in enumerate(((wq_hbm, wq), (wk_hbm, wk), (wv_hbm, wv), (wo_hbm, wo), (cw_hbm, cw)))
    ]
    for w in weights:
        w.start()
    first = jnp.minimum(tm, 1)
    cache_two = pltpu.make_async_copy(cache_hbm.at[first], cb.at[0, pl.ds(1, R)], s_loc.at[6])
    cache_one = pltpu.make_async_copy(cache_hbm.at[1], cb.at[1, pl.ds(1, R)], s_loc.at[7])
    pl.when(tm <= 1)(cache_two.start)
    pl.when(tm == 0)(cache_one.start)

    want = 1 + jnp.where(z > 0, 1, 0) + jnp.where(z < Z - 1, 1, 0) + jnp.where(has_near, 1, 0)
    for hop in (1, 2):
        if N > hop:
            want = want + jnp.where(tm + hop < N, 1, 0)
    pl.semaphore_wait(barrier, want)

    pair = send(x_hbm.at[0, pl.ds(o * hr, hr)], xr.at[c], s_pair.at[0], r_pair.at[0], dev(core=o))
    pair.start()

    blank = jnp.zeros((W, C), BF16)

    @pl.when(z == 0)
    def _():
        for f in range(3):
            cb[f, 0] = blank

    @pl.when(z == Z - 1)
    def _():
        for f in range(3):
            cb[f, R + 1] = blank

    x_own.wait()
    pair.wait_recv()

    def tokens():
        return jnp.concatenate(
            [xr[0].reshape(half, S).astype(F32), xr[1].reshape(half, S).astype(F32)], axis=-1
        )

    normed = normalized(tokens(), g1_ref[...]).astype(BF16)
    xg[z, c] = normed

    def rightward(j):
        return send(xg.at[j, c], xg.at[j, c], s_right.at[j], r_z.at[j], dev(dz=z + 1))

    def leftward(j):
        return send(xg.at[j, c], xg.at[j, c], s_left.at[j], r_z.at[j], dev(dz=z - 1))

    def sideward(j):
        return send(xg.at[j, c], xg.at[j, c], s_sib.at[j], r_sib.at[j], dev(core=o))

    pl.when(z < Z - 1)(rightward(z).start)
    pl.when(z > 0)(leftward(z).start)
    sideward(z).start()

    for w in weights[:2]:
        w.wait()
    query = jnp.dot(normed, wq[...], preferred_element_type=F32).astype(BF16)
    folded = lax.dot_general(query, wk[...], (((1,), (1,)), ((), ())), preferred_element_type=F32)
    qk[...] = (folded * (C ** (-0.5) * math.log2(math.e))).astype(BF16)
    top[...] = jnp.full(top.shape, -1e30, F32)
    total[...] = jnp.zeros(total.shape, F32)
    acc[...] = jnp.zeros(acc.shape, F32)

    def attend(j):
        keys = xg[j].reshape(T, C)
        scores = lax.dot_general(qk[...], keys, (((1,), (1,)), ((), ())), preferred_element_type=F32)
        old = top[...]
        new = jnp.maximum(old, jnp.max(scores, axis=-1, keepdims=True))
        weight = jnp.exp2(scores - new)
        fade = jnp.exp2(old - new)
        top[...] = new
        total[...] = total[...] * fade + jnp.sum(weight, axis=-1, keepdims=True)
        acc[...] = acc[...] * fade + jnp.dot(weight.astype(BF16), keys, preferred_element_type=F32)

    sideward(z).wait_recv()
    attend(z)

    def cache_edge(f, side):
        row = R - 1 if side == 0 else 0
        source = cache_hbm.at[first if f == 0 else 1, row]
        to = dev(dz=z + 1) if side == 0 else dev(dz=z - 1)
        return send(source, cb.at[f, 0 if side == 0 else R + 1], s_cache.at[f, side], r_halo.at[f, side], to)

    def cache_edges(act):
        for side, there in ((0, z < Z - 1), (1, z > 0)):
            pl.when(jnp.logical_and(there, tm <= 1))(lambda s=side: act(cache_edge(0, s)))
            pl.when(jnp.logical_and(there, tm == 0))(lambda s=side: act(cache_edge(1, s)))

    def step(d, carry):
        lo, hi = z - d, z + d
        has_lo, has_hi = lo >= 0, hi < Z

        @pl.when(has_lo)
        def _():
            rightward(lo).wait_recv()
            pl.when(z < Z - 1)(rightward(lo).start)
            sideward(lo).start()

        @pl.when(has_hi)
        def _():
            leftward(hi).wait_recv()
            pl.when(z > 0)(leftward(hi).start)
            sideward(hi).start()

        pl.when(d == Z - 1)(lambda: cache_edges(lambda copy: copy.start()))

        @pl.when(has_lo)
        def _():
            sideward(lo).wait_recv()
            attend(lo)

        @pl.when(has_hi)
        def _():
            sideward(hi).wait_recv()
            attend(hi)

        return carry

    lax.fori_loop(1, Z, step, 0)

    for w in weights[2:4]:
        w.wait()
    mixed = (acc[...] * (1.0 / total[...])).astype(BF16)
    attended = jnp.dot(mixed, wv[...], preferred_element_type=F32).astype(BF16)
    joined = tokens() + jnp.dot(attended, wo[...], preferred_element_type=F32)
    joined = joined.astype(BF16).astype(F32)
    scaled = normalized(joined, g2_ref[...])
    act = (scaled / (1.0 + jnp.exp(-scaled))).astype(BF16)
    mine = 1 + c * hr
    cb[2, pl.ds(mine, hr)] = act.reshape(hr, W, C)

    edge = jnp.where(c == 0, 1, R)
    rest = jnp.where(c == 0, 2, 1 + hr)
    far = jnp.where(c == 0, R + 1, 0)

    def along_tm(hop, part):
        row = cb.at[2, edge] if part == 0 else cb.at[2, pl.ds(rest, hr - 1)]
        there = cb.at[2 - hop, edge] if part == 0 else cb.at[2 - hop, pl.ds(rest, hr - 1)]
        return send(row, there, s_tm.at[hop - 1, part], r_tm.at[hop - 1, part], dev(frame=tm + hop))

    def edge_copy(f, k):
        src = cb.at[f, edge]
        if k == 0:
            return send(src, src, s_edge.at[f, 0], r_edge.at[f], dev(core=o))
        side = o
        return send(src, cb.at[f, far], s_edge.at[f, k], r_halo.at[f, side], dev(dz=near, core=k - 1))

    def rest_copy(f):
        src = cb.at[f, pl.ds(rest, hr - 1)]
        return send(src, src, s_rest.at[f], r_rest.at[f], dev(core=o))

    def from_sibling(f):
        there = jnp.where(c == 0, R, 1)
        others = jnp.where(c == 0, 1 + hr, 2)
        row = cb.at[f, there]
        send(row, row, s_edge.at[f, 0], r_edge.at[f], dev(core=o)).wait_recv()
        rows = cb.at[f, pl.ds(others, hr - 1)]
        send(rows, rows, s_rest.at[f], r_rest.at[f], dev(core=o)).wait_recv()

    def from_halo(f):
        @pl.when(z > 0)
        def _():
            row = cb.at[f, 0]
            send(row, row, s_edge.at[f, 1], r_halo.at[f, 0], dev(core=o)).wait_recv()

        @pl.when(z < Z - 1)
        def _():
            row = cb.at[f, R + 1]
            send(row, row, s_edge.at[f, 2], r_halo.at[f, 1], dev(core=o)).wait_recv()

    def spread_edge(f):
        edge_copy(f, 0).start()

        @pl.when(has_near)
        def _():
            edge_copy(f, 1).start()
            edge_copy(f, 2).start()

    for part in (0, 1):
        for hop in (1, 2):
            if N > hop:
                pl.when(tm + hop < N)(along_tm(hop, part).start)
        if part == 0:
            spread_edge(2)
        else:
            rest_copy(2).start()

    low, high = joined[:, :S].astype(BF16), joined[:, S:].astype(BF16)
    jo[pl.ds(c * hr, hr)] = jnp.where(c == 0, low, high).reshape(hr, W, S)
    jt[...] = jnp.where(c == 0, high, low).reshape(hr, W, S)
    joined_copy = send(jt, jo.at[pl.ds(c * hr, hr)], s_pair.at[1], r_pair.at[1], dev(core=o))
    joined_copy.start()

    def taps(f, start):
        rows = jnp.concatenate([cb[f, dh : dh + R].reshape(T, C) for dh in range(3)], axis=-1)
        for dw in range(3):
            value = jnp.dot(rows, cw[f, :, dw].reshape(3 * C, S), preferred_element_type=F32)
            if start:
                parts[dw, pl.ds(8, T)] = value
            else:
                parts[dw, pl.ds(8, T)] += value

    def forwarded(f):
        hop = 2 - f

        def run():
            for part in (0, 1):
                along_tm(hop, part).wait_recv()
                if part == 0:
                    spread_edge(f)
                else:
                    rest_copy(f).start()

        return run

    weights[4].wait()
    pl.when(tm <= 1)(cache_two.wait)
    from_sibling(2)
    from_halo(2)
    taps(2, True)
    if N > 2:
        pl.when(tm >= 2)(forwarded(0))
        pl.when(tm >= 2)(lambda: from_sibling(0))
    pl.when(tm >= 1)(forwarded(1))
    from_halo(0)
    taps(0, False)
    pl.when(tm == 0)(cache_one.wait)
    pl.when(tm >= 1)(lambda: from_sibling(1))
    from_halo(1)
    taps(1, False)

    there = jo.at[pl.ds(o * hr, hr)]
    send(jt, there, s_pair.at[1], r_pair.at[1], dev(core=o)).wait_recv()
    cell = lax.rem(lax.broadcasted_iota(jnp.int32, (T, S), 0), W)
    before = jnp.where(cell == 0, 0.0, parts[0, pl.ds(7, T)])
    after = jnp.where(cell == W - 1, 0.0, parts[2, pl.ds(9, T)])
    conv = before + parts[1, pl.ds(8, T)] + after
    out_ref[0] = (jo[...].reshape(T, S).astype(F32) + conv).astype(BF16).reshape(R, W, S)

    pair.wait_send()
    joined_copy.wait_send()
    pl.when(z < Z - 1)(rightward(z).wait_send)
    pl.when(z > 0)(leftward(z).wait_send)
    sideward(z).wait_send()

    def finish(d, carry):
        lo, hi = z - d, z + d

        @pl.when(lo >= 0)
        def _():
            pl.when(z < Z - 1)(rightward(lo).wait_send)
            sideward(lo).wait_send()

        @pl.when(hi < Z)
        def _():
            pl.when(z > 0)(leftward(hi).wait_send)
            sideward(hi).wait_send()

        return carry

    lax.fori_loop(1, Z, finish, 0)
    cache_edges(lambda copy: copy.wait_send())
    for part in (0, 1):
        for hop in (1, 2):
            if N > hop:
                pl.when(tm + hop < N)(along_tm(hop, part).wait_send)

    def spread_done(f):
        edge_copy(f, 0).wait_send()
        rest_copy(f).wait_send()

        @pl.when(has_near)
        def _():
            edge_copy(f, 1).wait_send()
            edge_copy(f, 2).wait_send()

    spread_done(2)
    pl.when(tm >= 1)(lambda: spread_done(1))
    if N > 2:
        pl.when(tm >= 2)(lambda: spread_done(0))


def solution(mesh):
    Z, N = mesh.shape["space"], mesh.shape["tm"]

    def body(frames_in, cache, gain_one, gain_two, w_query, w_key, w_value, w_out, conv_weight):
        _, R, W, S = frames_in.shape
        C = 2 * S
        hr, half, T = R // 2, R // 2 * W, R * W
        dma = pltpu.SemaphoreType.DMA
        hbm = pl.BlockSpec(memory_space=pl.ANY)
        vmem = pl.BlockSpec(memory_space=pltpu.VMEM)
        return pl.pallas_call(
            functools.partial(kernel, Z, N),
            out_shape=jax.ShapeDtypeStruct(frames_in.shape, BF16),
            in_specs=[hbm, hbm, vmem, vmem, hbm, hbm, hbm, hbm, hbm],
            out_specs=vmem,
            scratch_shapes=[
                pltpu.VMEM((2, hr, W, S), BF16),
                pltpu.VMEM((Z, 2, half, C), BF16),
                pltpu.VMEM((half, C), BF16),
                pltpu.VMEM((half, 1), F32),
                pltpu.VMEM((half, 1), F32),
                pltpu.VMEM((half, C), F32),
                pltpu.VMEM((3, R + 2, W, C), BF16),
                pltpu.VMEM((hr, W, S), BF16),
                pltpu.VMEM((R, W, S), BF16),
                pltpu.VMEM((3, T + 16, S), F32),
                pltpu.VMEM((C, C), BF16),
                pltpu.VMEM((C, C), BF16),
                pltpu.VMEM((C, C), BF16),
                pltpu.VMEM((C, C), BF16),
                pltpu.VMEM(conv_weight.shape, BF16),
                dma((8,)),
                dma((2,)),
                dma((2,)),
                dma((Z,)),
                dma((Z,)),
                dma((Z,)),
                dma((Z,)),
                dma((Z,)),
                dma((2, 2)),
                dma((3, 2)),
                dma((3, 3)),
                dma((3,)),
                dma((3,)),
                dma((3,)),
                dma((2, 2)),
                dma((2, 2)),
            ],
            compiler_params=pltpu.CompilerParams(
                collective_id=0, has_side_effects=True, vmem_limit_bytes=50 << 20
            ),
        )(
            frames_in, cache, gain_one.reshape(1, C), gain_two.reshape(1, C),
            w_query, w_key, w_value, w_out, conv_weight,
        )

    return jax.shard_map(
        body,
        mesh=mesh,
        in_specs=(
            P(("clips", "tm"), "space", None, "chan"),
            P("clips", "space", None, None),
            P(),
            P(),
            P(),
            P(),
            P(),
            P(),
            P(None, None, None, None, "chan"),
        ),
        out_specs=P(("clips", "tm"), "space", None, "chan"),
        check_vma=False,
    )
```

time: 117 us -> 53.5 us (0.46)
  the two profiles are of different devices: /device:TPU:0 before, /device:TPU:3 now
where the time goes in v1:
time: 53.5 us; the launch traced here: 53.2 us
  Pallas kernels  42.8 us (80%)
  local copies, waits for them, and re-layouts  10.4 us (19%)
    pallas_call x1, Pallas kernels, body(): pl.pallas_call(functools.partial(kernel, Z, N), out_shape=jax.ShapeDtypeS...  42.8 us
    unnamed x14, local copies, waits for them, and re-layouts  8.9 us

profile of v1, /device:TPU:3, one launch (start us, length us, event | category | flops | bytes accessed | tf_op | source)
XLA Modules:
  0.0 53.2 jit_solution(5685954664546137262)
XLA Ops:
  0.0 0.0 copy-start.5
  0.0 0.0 copy-start.4
  0.0 0.0 copy-start.3
  0.0 0.0 copy-start.2
  0.0 0.0 copy-start
  0.0 0.0 copy-start.1
  0.0 0.8 %reshape.6.g1_ref = bf16[1,384]{1,0:T(2,128)(2,1)S(1)} reshape(bf16[384]{0:T(512)(128)(2,1)} %param.11) | data formatting | bytes 1536 | tf_op jit(solution)/shard_map/reshape | solution.py:407
  0.9 0.7 %reshape.7.g2_ref = bf16[1,384]{1,0:T(2,128)(2,1)S(1)} reshape(bf16[384]{0:T(512)(128)(2,1)} %param.12) | data formatting | bytes 1536 | tf_op jit(solution)/shard_map/reshape | solution.py:407
  1.6 8.2 %copy.10.cw_hbm = bf16[3,3,3,384,192]{4,3,2,1,0:T(8,128)(2,1)} copy(bf16[3,3,3,384,192]{3,4,2,1,0:T(8,128)(2,1)} %param.17) | data formatting | bytes 7962624 | tf_op args[8]
  9.7 0.0 copy-done.5
  9.7 0.0 copy-done.4
  9.7 0.0 copy-done.3
  9.7 0.0 copy-done.2
  9.7 0.0 copy-done
  9.7 0.0 copy-done.1
  9.7 42.8 %shard_map.91 = bf16[1,4,160,192]{3,2,1,0:T(8,128)(2,1)S(1)} custom-call(bf16[1,4,160,192]{3,2,1,0:T(8,128)(2,1)S(1)} %copy-done.1, bf16[2,4,160,384]{3,2,1,0:T(8,128)(2,1)S(1)} %copy-done, bf16[1,384]{1,0:T(2,128)(2,1)S(1)} %reshape.6.g1_ref, bf16[1,384]{1,0:T(2,128)(2,1)S(1)} %reshape.7.g2_ref, bf16[384,384]{1,0:T(8,128)(2,1)S(1)} %copy-done.2, ...), custom_call_target="tpu_custom_call" | custom-call | tf_op jit(solution)/shard_map/pallas_call | solution.py:365
  52.5 0.7 %copy.12 = bf16[1,4,160,192]{3,2,1,0:T(8,128)(2,1)} copy(bf16[1,4,160,192]{3,2,1,0:T(8,128)(2,1)S(1)} %shard_map.91) | data formatting | bytes 491520
Async XLA Ops:
  0.0 9.7 %copy-start.5 = (bf16[384,384]{1,0:T(8,128)(2,1)S(1)}, bf16[384,384]{1,0:T(8,128)(2,1)}, u32[]{:S(2)}) copy-start(bf16[384,384]{1,0:T(8,128)(2,1)} %wo_hbm.1) | copy-start | bytes 884740
  0.0 9.7 %copy-start.4 = (bf16[384,384]{1,0:T(8,128)(2,1)S(1)}, bf16[384,384]{1,0:T(8,128)(2,1)}, u32[]{:S(2)}) copy-start(bf16[384,384]{1,0:T(8,128)(2,1)} %wv_hbm.1) | copy-start | bytes 884740
  0.0 9.7 %copy-start.3 = (bf16[384,384]{1,0:T(8,128)(2,1)S(1)}, bf16[384,384]{1,0:T(8,128)(2,1)}, u32[]{:S(2)}) copy-start(bf16[384,384]{1,0:T(8,128)(2,1)} %wk_hbm.1) | copy-start | bytes 884740
  0.0 9.7 %copy-start.2 = (bf16[384,384]{1,0:T(8,128)(2,1)S(1)}, bf16[384,384]{1,0:T(8,128)(2,1)}, u32[]{:S(2)}) copy-start(bf16[384,384]{1,0:T(8,128)(2,1)} %wq_hbm.1) | copy-start | bytes 884740
  0.0 9.7 %copy-start = (bf16[2,4,160,384]{3,2,1,0:T(8,128)(2,1)S(1)}, bf16[2,4,160,384]{3,2,1,0:T(8,128)(2,1)}, u32[]{:S(2)}) copy-start(bf16[2,4,160,384]{3,2,1,0:T(8,128)(2,1)} %cache_hbm.1) | copy-start | bytes 2949124
  0.0 9.7 %copy-start.1 = (bf16[1,4,160,192]{3,2,1,0:T(8,128)(2,1)S(1)}, bf16[1,4,160,192]{3,2,1,0:T(8,128)(2,1)}, u32[]{:S(2)}) copy-start(bf16[1,4,160,192]{3,2,1,0:T(8,128)(2,1)} %x_hbm.1) | copy-start | bytes 737284

commit v2 on v1

--- a/solution.py
+++ b/solution.py
@@ -15,14 +15,14 @@
 
 def normalized(wide, gain):
     factor = lax.rsqrt(jnp.mean(wide * wide, axis=-1, keepdims=True) + 1e-06)
-    return wide * factor * gain.astype(F32)
+    return wide * factor * gain.astype(F32).reshape(1, -1)
 
 
 def kernel(
     Z, N,
-    x_hbm, cache_hbm, g1_ref, g2_ref, wq_hbm, wk_hbm, wv_hbm, wo_hbm, cw_hbm,
+    x_hbm, cache_hbm, g1_hbm, g2_hbm, wq_hbm, wk_hbm, wv_hbm, wo_hbm, cw_hbm,
     out_ref,
-    xr, xg, qk, top, total, acc, cb, jt, jo, parts, wq, wk, wv, wo, cw,
+    xr, xg, qk, top, total, acc, cb, jt, jo, parts, g1_ref, g2_ref, wq, wk, wv, wo, cw,
     s_loc, s_pair, r_pair, s_right, s_left, s_sib, r_z, r_sib,
     s_cache, r_halo, s_edge, s_rest, r_edge, r_rest, s_tm, r_tm,
 ):
@@ -67,15 +67,19 @@
 
     x_own = pltpu.make_async_copy(x_hbm.at[0, pl.ds(c * hr, hr)], xr.at[c], s_loc.at[0])
     x_own.start()
+    pieces = (
+        (g1_hbm, g1_ref), (wq_hbm, wq), (wk_hbm, wk), (wv_hbm, wv), (wo_hbm, wo), (g2_hbm, g2_ref),
+        (cw_hbm, cw),
+    )
     weights = [
         pltpu.make_async_copy(a, b, s_loc.at[1 + i])
-        for i, (a, b) in enumerate(((wq_hbm, wq), (wk_hbm, wk), (wv_hbm, wv), (wo_hbm, wo), (cw_hbm, cw)))
+        for i, (a, b) in enumerate(pieces)
     ]
     for w in weights:
         w.start()
     first = jnp.minimum(tm, 1)
-    cache_two = pltpu.make_async_copy(cache_hbm.at[first], cb.at[0, pl.ds(1, R)], s_loc.at[6])
-    cache_one = pltpu.make_async_copy(cache_hbm.at[1], cb.at[1, pl.ds(1, R)], s_loc.at[7])
+    cache_two = pltpu.make_async_copy(cache_hbm.at[first], cb.at[0, pl.ds(1, R)], s_loc.at[8])
+    cache_one = pltpu.make_async_copy(cache_hbm.at[1], cb.at[1, pl.ds(1, R)], s_loc.at[9])
     pl.when(tm <= 1)(cache_two.start)
     pl.when(tm == 0)(cache_one.start)
 
@@ -101,6 +105,7 @@
             cb[f, R + 1] = blank
 
     x_own.wait()
+    weights[0].wait()
     pair.wait_recv()
 
     def tokens():
@@ -124,7 +129,7 @@
     pl.when(z > 0)(leftward(z).start)
     sideward(z).start()
 
-    for w in weights[:2]:
+    for w in weights[1:3]:
         w.wait()
     query = jnp.dot(normed, wq[...], preferred_element_type=F32).astype(BF16)
     folded = lax.dot_general(query, wk[...], (((1,), (1,)), ((), ())), preferred_element_type=F32)
@@ -190,7 +195,7 @@
 
     lax.fori_loop(1, Z, step, 0)
 
-    for w in weights[2:4]:
+    for w in weights[3:6]:
         w.wait()
     mixed = (acc[...] * (1.0 / total[...])).astype(BF16)
     attended = jnp.dot(mixed, wv[...], preferred_element_type=F32).astype(BF16)
@@ -266,7 +271,10 @@
     def taps(f, start):
         rows = jnp.concatenate([cb[f, dh : dh + R].reshape(T, C) for dh in range(3)], axis=-1)
         for dw in range(3):
-            value = jnp.dot(rows, cw[f, :, dw].reshape(3 * C, S), preferred_element_type=F32)
+            kernel_rows = jnp.concatenate([cw[f, dh, dw] for dh in range(3)], axis=-1)
+            value = lax.dot_general(
+                rows, kernel_rows, (((1,), (1,)), ((), ())), preferred_element_type=F32
+            )
             if start:
                 parts[dw, pl.ds(8, T)] = value
             else:
@@ -285,7 +293,7 @@
 
         return run
 
-    weights[4].wait()
+    weights[6].wait()
     pl.when(tm <= 1)(cache_two.wait)
     from_sibling(2)
     from_halo(2)
@@ -360,12 +368,12 @@
         C = 2 * S
         hr, half, T = R // 2, R // 2 * W, R * W
         dma = pltpu.SemaphoreType.DMA
-        hbm = pl.BlockSpec(memory_space=pl.ANY)
+        hbm = pl.BlockSpec(memory_space=pltpu.HBM)
         vmem = pl.BlockSpec(memory_space=pltpu.VMEM)
         return pl.pallas_call(
             functools.partial(kernel, Z, N),
             out_shape=jax.ShapeDtypeStruct(frames_in.shape, BF16),
-            in_specs=[hbm, hbm, vmem, vmem, hbm, hbm, hbm, hbm, hbm],
+            in_specs=[hbm] * 9,
             out_specs=vmem,
             scratch_shapes=[
                 pltpu.VMEM((2, hr, W, S), BF16),
@@ -378,12 +386,14 @@
                 pltpu.VMEM((hr, W, S), BF16),
                 pltpu.VMEM((R, W, S), BF16),
                 pltpu.VMEM((3, T + 16, S), F32),
+                pltpu.VMEM((C,), BF16),
+                pltpu.VMEM((C,), BF16),
                 pltpu.VMEM((C, C), BF16),
                 pltpu.VMEM((C, C), BF16),
                 pltpu.VMEM((C, C), BF16),
                 pltpu.VMEM((C, C), BF16),
-                pltpu.VMEM(conv_weight.shape, BF16),
-                dma((8,)),
+                pltpu.VMEM((3, 3, 3, S, C), BF16),
+                dma((10,)),
                 dma((2,)),
                 dma((2,)),
                 dma((Z,)),
@@ -401,11 +411,11 @@
                 dma((2, 2)),
             ],
             compiler_params=pltpu.CompilerParams(
-                collective_id=0, has_side_effects=True, vmem_limit_bytes=50 << 20
+                collective_id=0, has_side_effects=True, vmem_limit_bytes=63 << 20
             ),
         )(
-            frames_in, cache, gain_one.reshape(1, C), gain_two.reshape(1, C),
-            w_query, w_key, w_value, w_out, conv_weight,
+            frames_in, cache, gain_one, gain_two,
+            w_query, w_key, w_value, w_out, jnp.swapaxes(conv_weight, 3, 4),
         )
 
     return jax.shard_map(

time: 53.5 us -> 44.8 us (0.84)
  local copies, waits for them, and re-layouts: 10.4 us -> 1.72 us
    unnamed x14 -> x1, local copies, waits for them, and re-layouts: 8.9 us -> 1.72 us
    reshape x2 -> x0, local copies, waits for them, and re-layouts: 1.51 us -> none  [the longest x1 0.83 us: body(): gain_one.reshape(1, C)]
where the time goes in v2:
time: 44.8 us; the launch traced here: 44.7 us
  Pallas kernels  42.9 us (96%)
  local copies, waits for them, and re-layouts  1.72 us (4%)
    pallas_call x1, Pallas kernels, body(): pl.pallas_call(functools.partial(kernel, Z, N), out_shape=jax.ShapeDtypeS...  42.9 us
    unnamed x1, local copies, waits for them, and re-layouts  1.72 us

profile of v2, /device:TPU:3, one launch (start us, length us, event | category | flops | bytes accessed | tf_op | source)
XLA Modules:
  0.0 44.7 jit_solution(13458367099881694658)
XLA Ops:
  0.0 42.9 %shard_map.91 = bf16[1,4,160,192]{3,2,1,0:T(8,128)(2,1)} custom-call(bf16[1,4,160,192]{3,2,1,0:T(8,128)(2,1)} %x_hbm.1, bf16[2,4,160,384]{3,2,1,0:T(8,128)(2,1)} %cache_hbm.1, bf16[384]{0:T(512)(128)(2,1)} %g1_hbm.1, bf16[384]{0:T(512)(128)(2,1)} %g2_hbm.1, bf16[384,384]{1,0:T(8,128)(2,1)} %wq_hbm.1, bf16[384,384]{1,0:T(8,128)(2,1)} %wk_hbm.1, ...), custom_call_target="tpu_custom_call" | custom-call | tf_op jit(solution)/shard_map/pallas_call | solution.py:373
  42.9 1.7 %copy.11 = bf16[1,4,160,192]{3,2,1,0:T(8,128)(2,1)} copy(bf16[1,4,160,192]{3,2,1,0:T(8,128)(2,1)} %shard_map.91) | data formatting | bytes 491520

commit v3 on v2

--- a/solution.py
+++ b/solution.py
@@ -24,7 +24,7 @@
     out_ref,
     xr, xg, qk, top, total, acc, cb, jt, jo, parts, g1_ref, g2_ref, wq, wk, wv, wo, cw,
     s_loc, s_pair, r_pair, s_right, s_left, s_sib, r_z, r_sib,
-    s_cache, r_halo, s_edge, s_rest, r_edge, r_rest, s_tm, r_tm,
+    s_cache, r_halo, s_edge, s_rest, r_edge, r_rest, s_tm, r_tm, s_half, r_half,
 ):
     z = lax.axis_index("space")
     c = lax.axis_index("chan")
@@ -35,6 +35,7 @@
     hr = R // 2
     half = hr * W
     T = R * W
+    hw = W // 2
 
     def dev(dz=None, core=None, frame=None):
         return {
@@ -108,26 +109,29 @@
     weights[0].wait()
     pair.wait_recv()
 
-    def tokens():
+    def tokens(row, count):
+        at = pl.ds(row, count)
         return jnp.concatenate(
-            [xr[0].reshape(half, S).astype(F32), xr[1].reshape(half, S).astype(F32)], axis=-1
+            [xr[k, at].reshape(count * W, S).astype(F32) for k in range(2)], axis=-1
         )
 
-    normed = normalized(tokens(), g1_ref[...]).astype(BF16)
-    xg[z, c] = normed
-
-    def rightward(j):
-        return send(xg.at[j, c], xg.at[j, c], s_right.at[j], r_z.at[j], dev(dz=z + 1))
-
-    def leftward(j):
-        return send(xg.at[j, c], xg.at[j, c], s_left.at[j], r_z.at[j], dev(dz=z - 1))
-
-    def sideward(j):
-        return send(xg.at[j, c], xg.at[j, c], s_sib.at[j], r_sib.at[j], dev(core=o))
-
-    pl.when(z < Z - 1)(rightward(z).start)
-    pl.when(z > 0)(leftward(z).start)
-    sideward(z).start()
+    normed = normalized(tokens(0, hr), g1_ref[...]).astype(BF16)
+    xg[z, c] = normed.reshape(hr, W, C)
+
+    def rightward(j, r):
+        return send(xg.at[j, c, r], xg.at[j, c, r], s_right.at[j, r], r_z.at[j, r], dev(dz=z + 1))
+
+    def leftward(j, r):
+        return send(xg.at[j, c, r], xg.at[j, c, r], s_left.at[j, r], r_z.at[j, r], dev(dz=z - 1))
+
+    def sideward(j, r):
+        return send(xg.at[j, c, r], xg.at[j, c, r], s_sib.at[j, r], r_sib.at[j, r], dev(core=o))
+
+    for r in range(hr):
+        pl.when(z < Z - 1)(rightward(z, r).start)
+        pl.when(z > 0)(leftward(z, r).start)
+    for r in range(hr):
+        sideward(z, r).start()
 
     for w in weights[1:3]:
         w.wait()
@@ -149,14 +153,16 @@
         total[...] = total[...] * fade + jnp.sum(weight, axis=-1, keepdims=True)
         acc[...] = acc[...] * fade + jnp.dot(weight.astype(BF16), keys, preferred_element_type=F32)
 
-    sideward(z).wait_recv()
+    for r in range(hr):
+        sideward(z, r).wait_recv()
     attend(z)
 
     def cache_edge(f, side):
         row = R - 1 if side == 0 else 0
-        source = cache_hbm.at[first if f == 0 else 1, row]
+        cells = pl.ds(pl.multiple_of(c * hw, hw), hw)
+        source = cache_hbm.at[first if f == 0 else 1, row, cells]
         to = dev(dz=z + 1) if side == 0 else dev(dz=z - 1)
-        return send(source, cb.at[f, 0 if side == 0 else R + 1], s_cache.at[f, side], r_halo.at[f, side], to)
+        return send(source, cb.at[f, 0 if side == 0 else R + 1, cells], s_cache.at[f, side], r_halo.at[f, side], to)
 
     def cache_edges(act):
         for side, there in ((0, z < Z - 1), (1, z > 0)):
@@ -167,28 +173,32 @@
         lo, hi = z - d, z + d
         has_lo, has_hi = lo >= 0, hi < Z
 
+        for r in range(hr):
+
+            @pl.when(has_lo)
+            def _():
+                rightward(lo, r).wait_recv()
+                pl.when(z < Z - 1)(rightward(lo, r).start)
+                sideward(lo, r).start()
+
+            @pl.when(has_hi)
+            def _():
+                leftward(hi, r).wait_recv()
+                pl.when(z > 0)(leftward(hi, r).start)
+                sideward(hi, r).start()
+
+        pl.when(d == Z - 1)(lambda: cache_edges(lambda copy: copy.start()))
+
         @pl.when(has_lo)
         def _():
-            rightward(lo).wait_recv()
-            pl.when(z < Z - 1)(rightward(lo).start)
-            sideward(lo).start()
+            for r in range(hr):
+                sideward(lo, r).wait_recv()
+            attend(lo)
 
         @pl.when(has_hi)
         def _():
-            leftward(hi).wait_recv()
-            pl.when(z > 0)(leftward(hi).start)
-            sideward(hi).start()
-
-        pl.when(d == Z - 1)(lambda: cache_edges(lambda copy: copy.start()))
-
-        @pl.when(has_lo)
-        def _():
-            sideward(lo).wait_recv()
-            attend(lo)
-
-        @pl.when(has_hi)
-        def _():
-            sideward(hi).wait_recv()
+            for r in range(hr):
+                sideward(hi, r).wait_recv()
             attend(hi)
 
         return carry
@@ -197,14 +207,18 @@
 
     for w in weights[3:6]:
         w.wait()
-    mixed = (acc[...] * (1.0 / total[...])).astype(BF16)
-    attended = jnp.dot(mixed, wv[...], preferred_element_type=F32).astype(BF16)
-    joined = tokens() + jnp.dot(attended, wo[...], preferred_element_type=F32)
-    joined = joined.astype(BF16).astype(F32)
-    scaled = normalized(joined, g2_ref[...])
-    act = (scaled / (1.0 + jnp.exp(-scaled))).astype(BF16)
-    mine = 1 + c * hr
-    cb[2, pl.ds(mine, hr)] = act.reshape(hr, W, C)
+    def finish_rows(row, count):
+        at = pl.ds(pl.multiple_of(row * W, W), count * W)
+        mixed = (acc[at, :] * (1.0 / total[at, :])).astype(BF16)
+        attended = jnp.dot(mixed, wv[...], preferred_element_type=F32).astype(BF16)
+        joined = tokens(row, count) + jnp.dot(attended, wo[...], preferred_element_type=F32)
+        joined = joined.astype(BF16).astype(F32)
+        scaled = normalized(joined, g2_ref[...])
+        act = (scaled / (1.0 + jnp.exp(-scaled))).astype(BF16)
+        cb[2, pl.ds(1 + c * hr + row, count)] = act.reshape(count, W, C)
+        low, high = joined[:, :S].astype(BF16), joined[:, S:].astype(BF16)
+        jo[pl.ds(c * hr + row, count)] = jnp.where(c == 0, low, high).reshape(count, W, S)
+        jt[pl.ds(row, count)] = jnp.where(c == 0, high, low).reshape(count, W, S)
 
     edge = jnp.where(c == 0, 1, R)
     rest = jnp.where(c == 0, 2, 1 + hr)
@@ -219,8 +233,11 @@
         src = cb.at[f, edge]
         if k == 0:
             return send(src, src, s_edge.at[f, 0], r_edge.at[f], dev(core=o))
-        side = o
-        return send(src, cb.at[f, far], s_edge.at[f, k], r_halo.at[f, side], dev(dz=near, core=k - 1))
+        cells = pl.ds((k - 1) * hw, hw)
+        return send(
+            cb.at[f, edge, cells], cb.at[f, far, cells], s_edge.at[f, k], r_halo.at[f, o],
+            dev(dz=near, core=k - 1),
+        )
 
     def rest_copy(f):
         src = cb.at[f, pl.ds(rest, hr - 1)]
@@ -234,16 +251,24 @@
         rows = cb.at[f, pl.ds(others, hr - 1)]
         send(rows, rows, s_rest.at[f], r_rest.at[f], dev(core=o)).wait_recv()
 
+    def halo_half(f, side, core):
+        half_row = cb.at[f, 0 if side == 0 else R + 1, pl.ds(pl.multiple_of(core * hw, hw), hw)]
+        return send(half_row, half_row, s_half.at[f, side], r_half.at[f, side], dev(core=o))
+
+    def both_sides(visit):
+        pl.when(z > 0)(lambda: visit(0))
+        pl.when(z < Z - 1)(lambda: visit(1))
+
+    def relay_halo(f):
+        def visit(side):
+            half_row = cb.at[f, 0 if side == 0 else R + 1, pl.ds(pl.multiple_of(c * hw, hw), hw)]
+            send(half_row, half_row, s_edge.at[f, 1], r_halo.at[f, side], dev(core=o)).wait_recv()
+            halo_half(f, side, c).start()
+
+        both_sides(visit)
+
     def from_halo(f):
-        @pl.when(z > 0)
-        def _():
-            row = cb.at[f, 0]
-            send(row, row, s_edge.at[f, 1], r_halo.at[f, 0], dev(core=o)).wait_recv()
-
-        @pl.when(z < Z - 1)
-        def _():
-            row = cb.at[f, R + 1]
-            send(row, row, s_edge.at[f, 2], r_halo.at[f, 1], dev(core=o)).wait_recv()
+        both_sides(lambda side: halo_half(f, side, o).wait_recv())
 
     def spread_edge(f):
         edge_copy(f, 0).start()
@@ -254,6 +279,10 @@
             edge_copy(f, 2).start()
 
     for part in (0, 1):
+        if part == 0:
+            finish_rows(edge - 1 - c * hr, 1)
+        else:
+            finish_rows(rest - 1 - c * hr, hr - 1)
         for hop in (1, 2):
             if N > hop:
                 pl.when(tm + hop < N)(along_tm(hop, part).start)
@@ -262,9 +291,6 @@
         else:
             rest_copy(2).start()
 
-    low, high = joined[:, :S].astype(BF16), joined[:, S:].astype(BF16)
-    jo[pl.ds(c * hr, hr)] = jnp.where(c == 0, low, high).reshape(hr, W, S)
-    jt[...] = jnp.where(c == 0, high, low).reshape(hr, W, S)
     joined_copy = send(jt, jo.at[pl.ds(c * hr, hr)], s_pair.at[1], r_pair.at[1], dev(core=o))
     joined_copy.start()
 
@@ -280,32 +306,40 @@
             else:
                 parts[dw, pl.ds(8, T)] += value
 
-    def forwarded(f):
-        hop = 2 - f
-
-        def run():
-            for part in (0, 1):
-                along_tm(hop, part).wait_recv()
-                if part == 0:
-                    spread_edge(f)
-                else:
-                    rest_copy(f).start()
-
-        return run
-
+    def forwarded(f, part):
+        along_tm(2 - f, part).wait_recv()
+        if part == 0:
+            spread_edge(f)
+        else:
+            rest_copy(f).start()
+
+    def arrived(f):
+        relay_halo(f)
+        from_sibling(f)
+
+    def older():
+        forwarded(0, 0)
+        forwarded(0, 1)
+        arrived(0)
+
+    def newer():
+        forwarded(1, 1)
+        arrived(1)
+
+    pl.when(tm <= 1)(lambda: relay_halo(0))
+    pl.when(tm == 0)(lambda: relay_halo(1))
+    arrived(2)
     weights[6].wait()
     pl.when(tm <= 1)(cache_two.wait)
-    from_sibling(2)
+    pl.when(tm == 0)(cache_one.wait)
     from_halo(2)
     taps(2, True)
     if N > 2:
-        pl.when(tm >= 2)(forwarded(0))
-        pl.when(tm >= 2)(lambda: from_sibling(0))
-    pl.when(tm >= 1)(forwarded(1))
+        pl.when(tm >= 2)(older)
+    pl.when(tm >= 1)(lambda: forwarded(1, 0))
     from_halo(0)
     taps(0, False)
-    pl.when(tm == 0)(cache_one.wait)
-    pl.when(tm >= 1)(lambda: from_sibling(1))
+    pl.when(tm >= 1)(newer)
     from_halo(1)
     taps(1, False)
 
@@ -319,27 +353,32 @@
 
     pair.wait_send()
     joined_copy.wait_send()
-    pl.when(z < Z - 1)(rightward(z).wait_send)
-    pl.when(z > 0)(leftward(z).wait_send)
-    sideward(z).wait_send()
+    for r in range(hr):
+        pl.when(z < Z - 1)(rightward(z, r).wait_send)
+        pl.when(z > 0)(leftward(z, r).wait_send)
+        sideward(z, r).wait_send()
 
     def finish(d, carry):
         lo, hi = z - d, z + d
 
-        @pl.when(lo >= 0)
-        def _():
-            pl.when(z < Z - 1)(rightward(lo).wait_send)
-            sideward(lo).wait_send()
-
-        @pl.when(hi < Z)
-        def _():
-            pl.when(z > 0)(leftward(hi).wait_send)
-            sideward(hi).wait_send()
+        for r in range(hr):
+
+            @pl.when(lo >= 0)
+            def _():
+                pl.when(z < Z - 1)(rightward(lo, r).wait_send)
+                sideward(lo, r).wait_send()
+
+            @pl.when(hi < Z)
+            def _():
+                pl.when(z > 0)(leftward(hi, r).wait_send)
+                sideward(hi, r).wait_send()
 
         return carry
 
     lax.fori_loop(1, Z, finish, 0)
     cache_edges(lambda copy: copy.wait_send())
+    for f in range(3):
+        both_sides(lambda side: halo_half(f, side, c).wait_send())
     for part in (0, 1):
         for hop in (1, 2):
             if N > hop:
@@ -377,7 +416,7 @@
             out_specs=vmem,
             scratch_shapes=[
                 pltpu.VMEM((2, hr, W, S), BF16),
-                pltpu.VMEM((Z, 2, half, C), BF16),
+                pltpu.VMEM((Z, 2, hr, W, C), BF16),
                 pltpu.VMEM((half, C), BF16),
                 pltpu.VMEM((half, 1), F32),
                 pltpu.VMEM((half, 1), F32),
@@ -396,11 +435,11 @@
                 dma((10,)),
                 dma((2,)),
                 dma((2,)),
-                dma((Z,)),
-                dma((Z,)),
-                dma((Z,)),
-                dma((Z,)),
-                dma((Z,)),
+                dma((Z, hr)),
+                dma((Z, hr)),
+                dma((Z, hr)),
+                dma((Z, hr)),
+                dma((Z, hr)),
                 dma((2, 2)),
                 dma((3, 2)),
                 dma((3, 3)),
@@ -409,6 +448,8 @@
                 dma((3,)),
                 dma((2, 2)),
                 dma((2, 2)),
+                dma((3, 2)),
+                dma((3, 2)),
             ],
             compiler_params=pltpu.CompilerParams(
                 collective_id=0, has_side_effects=True, vmem_limit_bytes=63 << 20

time: 44.8 us -> 40.6 us (0.906)
  Pallas kernels: 42.9 us -> 38.7 us
    pallas_call x1, Pallas kernels: 42.9 us -> 38.7 us  [body(): pl.pallas_call(functools.partial(kernel, Z, N), out_shape=jax.ShapeDtypeS...]
where the time goes in v3:
time: 40.6 us; the launch traced here: 40.4 us
  Pallas kernels  38.7 us (95%)
  local copies, waits for them, and re-layouts  1.72 us (4%)
    pallas_call x1, Pallas kernels, body(): pl.pallas_call(functools.partial(kernel, Z, N), out_shape=jax.ShapeDtypeS...  38.7 us
    unnamed x1, local copies, waits for them, and re-layouts  1.72 us

profile of v3, /device:TPU:3, one launch (start us, length us, event | category | flops | bytes accessed | tf_op | source)
XLA Modules:
  0.0 40.4 jit_solution(3392508863781402714)
XLA Ops:
  0.0 38.7 %shard_map.91 = bf16[1,4,160,192]{3,2,1,0:T(8,128)(2,1)} custom-call(bf16[1,4,160,192]{3,2,1,0:T(8,128)(2,1)} %x_hbm.1, bf16[2,4,160,384]{3,2,1,0:T(8,128)(2,1)} %cache_hbm.1, bf16[384]{0:T(512)(128)(2,1)} %g1_hbm.1, bf16[384]{0:T(512)(128)(2,1)} %g2_hbm.1, bf16[384,384]{1,0:T(8,128)(2,1)} %wq_hbm.1, bf16[384,384]{1,0:T(8,128)(2,1)} %wk_hbm.1, ...), custom_call_target="tpu_custom_call" | custom-call | tf_op jit(solution)/shard_map/pallas_call | solution.py:412
  38.7 1.7 %copy.11 = bf16[1,4,160,192]{3,2,1,0:T(8,128)(2,1)} copy(bf16[1,4,160,192]{3,2,1,0:T(8,128)(2,1)} %shard_map.91) | data formatting | bytes 491520

commit v4 on v3

--- a/solution.py
+++ b/solution.py
@@ -23,7 +23,7 @@
     x_hbm, cache_hbm, g1_hbm, g2_hbm, wq_hbm, wk_hbm, wv_hbm, wo_hbm, cw_hbm,
     out_ref,
     xr, xg, qk, top, total, acc, cb, jt, jo, parts, g1_ref, g2_ref, wq, wk, wv, wo, cw,
-    s_loc, s_pair, r_pair, s_right, s_left, s_sib, r_z, r_sib,
+    s_loc, s_pair, r_pair, s_first, r_first, s_right, s_left, s_sib, r_z, r_sib,
     s_cache, r_halo, s_edge, s_rest, r_edge, r_rest, s_tm, r_tm, s_half, r_half,
 ):
     z = lax.axis_index("space")
@@ -90,8 +90,11 @@
             want = want + jnp.where(tm + hop < N, 1, 0)
     pl.semaphore_wait(barrier, want)
 
-    pair = send(x_hbm.at[0, pl.ds(o * hr, hr)], xr.at[c], s_pair.at[0], r_pair.at[0], dev(core=o))
-    pair.start()
+    def pair(r):
+        return send(x_hbm.at[0, o * hr + r], xr.at[c, r], s_first.at[r], r_first.at[r], dev(core=o))
+
+    for r in range(hr):
+        pair(r).start()
 
     blank = jnp.zeros((W, C), BF16)
 
@@ -107,17 +110,12 @@
 
     x_own.wait()
     weights[0].wait()
-    pair.wait_recv()
-
     def tokens(row, count):
         at = pl.ds(row, count)
         return jnp.concatenate(
             [xr[k, at].reshape(count * W, S).astype(F32) for k in range(2)], axis=-1
         )
 
-    normed = normalized(tokens(0, hr), g1_ref[...]).astype(BF16)
-    xg[z, c] = normed.reshape(hr, W, C)
-
     def rightward(j, r):
         return send(xg.at[j, c, r], xg.at[j, c, r], s_right.at[j, r], r_z.at[j, r], dev(dz=z + 1))
 
@@ -128,14 +126,16 @@
         return send(xg.at[j, c, r], xg.at[j, c, r], s_sib.at[j, r], r_sib.at[j, r], dev(core=o))
 
     for r in range(hr):
+        pair(r).wait_recv()
+        normed = normalized(tokens(r, 1), g1_ref[...]).astype(BF16)
+        xg[z, c, r] = normed.reshape(W, C)
         pl.when(z < Z - 1)(rightward(z, r).start)
         pl.when(z > 0)(leftward(z, r).start)
-    for r in range(hr):
         sideward(z, r).start()
 
     for w in weights[1:3]:
         w.wait()
-    query = jnp.dot(normed, wq[...], preferred_element_type=F32).astype(BF16)
+    query = jnp.dot(xg[z, c].reshape(half, C), wq[...], preferred_element_type=F32).astype(BF16)
     folded = lax.dot_general(query, wk[...], (((1,), (1,)), ((), ())), preferred_element_type=F32)
     qk[...] = (folded * (C ** (-0.5) * math.log2(math.e))).astype(BF16)
     top[...] = jnp.full(top.shape, -1e30, F32)
@@ -291,7 +291,7 @@
         else:
             rest_copy(2).start()
 
-    joined_copy = send(jt, jo.at[pl.ds(c * hr, hr)], s_pair.at[1], r_pair.at[1], dev(core=o))
+    joined_copy = send(jt, jo.at[pl.ds(c * hr, hr)], s_pair, r_pair, dev(core=o))
     joined_copy.start()
 
     def taps(f, start):
@@ -344,16 +344,16 @@
     taps(1, False)
 
     there = jo.at[pl.ds(o * hr, hr)]
-    send(jt, there, s_pair.at[1], r_pair.at[1], dev(core=o)).wait_recv()
+    send(jt, there, s_pair, r_pair, dev(core=o)).wait_recv()
     cell = lax.rem(lax.broadcasted_iota(jnp.int32, (T, S), 0), W)
     before = jnp.where(cell == 0, 0.0, parts[0, pl.ds(7, T)])
     after = jnp.where(cell == W - 1, 0.0, parts[2, pl.ds(9, T)])
     conv = before + parts[1, pl.ds(8, T)] + after
     out_ref[0] = (jo[...].reshape(T, S).astype(F32) + conv).astype(BF16).reshape(R, W, S)
 
-    pair.wait_send()
     joined_copy.wait_send()
     for r in range(hr):
+        pair(r).wait_send()
         pl.when(z < Z - 1)(rightward(z, r).wait_send)
         pl.when(z > 0)(leftward(z, r).wait_send)
         sideward(z, r).wait_send()
@@ -433,8 +433,10 @@
                 pltpu.VMEM((C, C), BF16),
                 pltpu.VMEM((3, 3, 3, S, C), BF16),
                 dma((10,)),
-                dma((2,)),
-                dma((2,)),
+                dma,
+                dma,
+                dma((hr,)),
+                dma((hr,)),
                 dma((Z, hr)),
                 dma((Z, hr)),
                 dma((Z, hr)),
@@ -452,12 +454,12 @@
                 dma((3, 2)),
             ],
             compiler_params=pltpu.CompilerParams(
-                collective_id=0, has_side_effects=True, vmem_limit_bytes=63 << 20
+                collective_id=0, has_side_effects=True, vmem_limit_bytes=50 << 20
             ),
-        )(
+        )(*(pltpu.with_memory_space_constraint(a, pltpu.HBM) for a in (
             frames_in, cache, gain_one, gain_two,
             w_query, w_key, w_value, w_out, jnp.swapaxes(conv_weight, 3, 4),
-        )
+        )))
 
     return jax.shard_map(
         body,

time: 40.6 us -> 38.7 us (0.953)
  local copies, waits for them, and re-layouts: 1.72 us -> 0.73 us
  Pallas kernels: 38.7 us -> 37.8 us
    unnamed x1, local copies, waits for them, and re-layouts: 1.72 us -> 0.73 us
    pallas_call x1, Pallas kernels: 38.7 us -> 37.8 us  [body(): pl.pallas_call(functools.partial(kernel, Z, N), out_shape=jax.ShapeDtypeS...]
where the time goes in v4:
time: 38.7 us; the launch traced here: 38.6 us
  Pallas kernels  37.8 us (98%)
  local copies, waits for them, and re-layouts  0.73 us (2%)
    pallas_call x1, Pallas kernels, body(): pl.pallas_call(functools.partial(kernel, Z, N), out_shape=jax.ShapeDtypeS...  37.8 us

profile of v4, /device:TPU:3, one launch (start us, length us, event | category | flops | bytes accessed | tf_op | source)
XLA Modules:
  0.0 38.6 jit_solution(11378372990180915327)
XLA Ops:
  0.0 37.8 %shard_map.91 = bf16[1,4,160,192]{3,2,1,0:T(8,128)(2,1)S(1)} custom-call(bf16[1,4,160,192]{3,2,1,0:T(8,128)(2,1)} %x_hbm.1, bf16[2,4,160,384]{3,2,1,0:T(8,128)(2,1)} %cache_hbm.1, bf16[384]{0:T(512)(128)(2,1)} %g1_hbm.1, bf16[384]{0:T(512)(128)(2,1)} %g2_hbm.1, bf16[384,384]{1,0:T(8,128)(2,1)} %wq_hbm.1, bf16[384,384]{1,0:T(8,128)(2,1)} %wk_hbm.1, ...), custom_call_target="tpu_custom_call" | custom-call | tf_op jit(solution)/shard_map/pallas_call | solution.py:412
  37.8 0.7 %copy.11 = bf16[1,4,160,192]{3,2,1,0:T(8,128)(2,1)} copy(bf16[1,4,160,192]{3,2,1,0:T(8,128)(2,1)S(1)} %shard_map.91) | data formatting | bytes 491520

commit v5 on v4

--- a/solution.py
+++ b/solution.py
@@ -117,33 +117,33 @@
         )
 
     def rightward(j, r):
-        return send(xg.at[j, c, r], xg.at[j, c, r], s_right.at[j, r], r_z.at[j, r], dev(dz=z + 1))
+        return send(xg.at[j, r, c], xg.at[j, r, c], s_right.at[j, r], r_z.at[j, r], dev(dz=z + 1))
 
     def leftward(j, r):
-        return send(xg.at[j, c, r], xg.at[j, c, r], s_left.at[j, r], r_z.at[j, r], dev(dz=z - 1))
+        return send(xg.at[j, r, c], xg.at[j, r, c], s_left.at[j, r], r_z.at[j, r], dev(dz=z - 1))
 
     def sideward(j, r):
-        return send(xg.at[j, c, r], xg.at[j, c, r], s_sib.at[j, r], r_sib.at[j, r], dev(core=o))
+        return send(xg.at[j, r, c], xg.at[j, r, c], s_sib.at[j, r], r_sib.at[j, r], dev(core=o))
 
     for r in range(hr):
         pair(r).wait_recv()
         normed = normalized(tokens(r, 1), g1_ref[...]).astype(BF16)
-        xg[z, c, r] = normed.reshape(W, C)
+        xg[z, r, c] = normed.reshape(W, C)
         pl.when(z < Z - 1)(rightward(z, r).start)
         pl.when(z > 0)(leftward(z, r).start)
         sideward(z, r).start()
 
     for w in weights[1:3]:
         w.wait()
-    query = jnp.dot(xg[z, c].reshape(half, C), wq[...], preferred_element_type=F32).astype(BF16)
+    query = jnp.dot(jnp.concatenate([xg[z, r, c] for r in range(hr)], axis=0), wq[...], preferred_element_type=F32).astype(BF16)
     folded = lax.dot_general(query, wk[...], (((1,), (1,)), ((), ())), preferred_element_type=F32)
     qk[...] = (folded * (C ** (-0.5) * math.log2(math.e))).astype(BF16)
     top[...] = jnp.full(top.shape, -1e30, F32)
     total[...] = jnp.zeros(total.shape, F32)
     acc[...] = jnp.zeros(acc.shape, F32)
 
-    def attend(j):
-        keys = xg[j].reshape(T, C)
+    def attend(j, r):
+        keys = xg[j, r].reshape(2 * W, C)
         scores = lax.dot_general(qk[...], keys, (((1,), (1,)), ((), ())), preferred_element_type=F32)
         old = top[...]
         new = jnp.maximum(old, jnp.max(scores, axis=-1, keepdims=True))
@@ -155,7 +155,7 @@
 
     for r in range(hr):
         sideward(z, r).wait_recv()
-    attend(z)
+        attend(z, r)
 
     def cache_edge(f, side):
         row = R - 1 if side == 0 else 0
@@ -187,19 +187,18 @@
                 pl.when(z > 0)(leftward(hi, r).start)
                 sideward(hi, r).start()
 
-        pl.when(d == Z - 1)(lambda: cache_edges(lambda copy: copy.start()))
-
-        @pl.when(has_lo)
-        def _():
-            for r in range(hr):
+            if r == hr - 1:
+                pl.when(d == Z - 1)(lambda: cache_edges(lambda copy: copy.start()))
+
+            @pl.when(has_lo)
+            def _():
                 sideward(lo, r).wait_recv()
-            attend(lo)
-
-        @pl.when(has_hi)
-        def _():
-            for r in range(hr):
+                attend(lo, r)
+
+            @pl.when(has_hi)
+            def _():
                 sideward(hi, r).wait_recv()
-            attend(hi)
+                attend(hi, r)
 
         return carry
 
@@ -416,7 +415,7 @@
             out_specs=vmem,
             scratch_shapes=[
                 pltpu.VMEM((2, hr, W, S), BF16),
-                pltpu.VMEM((Z, 2, hr, W, C), BF16),
+                pltpu.VMEM((Z, hr, 2, W, C), BF16),
                 pltpu.VMEM((half, C), BF16),
                 pltpu.VMEM((half, 1), F32),
                 pltpu.VMEM((half, 1), F32),

time: 38.7 us -> 38.7 us (level)
  no operation moved by 1% of the time
where the time goes in v5:
time: 38.7 us; the launch traced here: 38.6 us
  Pallas kernels  37.8 us (98%)
  local copies, waits for them, and re-layouts  0.73 us (2%)
    pallas_call x1, Pallas kernels, body(): pl.pallas_call(functools.partial(kernel, Z, N), out_shape=jax.ShapeDtypeS...  37.8 us

profile of v5, /device:TPU:3, one launch (start us, length us, event | category | flops | bytes accessed | tf_op | source)
XLA Modules:
  0.0 38.6 jit_solution(15219276316898080085)
XLA Ops:
  0.0 37.8 %shard_map.91 = bf16[1,4,160,192]{3,2,1,0:T(8,128)(2,1)S(1)} custom-call(bf16[1,4,160,192]{3,2,1,0:T(8,128)(2,1)} %x_hbm.1, bf16[2,4,160,384]{3,2,1,0:T(8,128)(2,1)} %cache_hbm.1, bf16[384]{0:T(512)(128)(2,1)} %g1_hbm.1, bf16[384]{0:T(512)(128)(2,1)} %g2_hbm.1, bf16[384,384]{1,0:T(8,128)(2,1)} %wq_hbm.1, bf16[384,384]{1,0:T(8,128)(2,1)} %wk_hbm.1, ...), custom_call_target="tpu_custom_call" | custom-call | tf_op jit(solution)/shard_map/pallas_call | solution.py:411
  37.8 0.7 %copy.11 = bf16[1,4,160,192]{3,2,1,0:T(8,128)(2,1)} copy(bf16[1,4,160,192]{3,2,1,0:T(8,128)(2,1)S(1)} %shard_map.91) | data formatting | bytes 491520

commit v6 on v5

--- a/solution.py
+++ b/solution.py
@@ -327,6 +327,9 @@
 
     pl.when(tm <= 1)(lambda: relay_halo(0))
     pl.when(tm == 0)(lambda: relay_halo(1))
+    inner = jnp.logical_and(z > 0, z < Z - 1)
+    outer = jnp.logical_or(z == 0, z == Z - 1)
+    pl.when(jnp.logical_and(tm >= 1, inner))(lambda: forwarded(1, 0))
     arrived(2)
     weights[6].wait()
     pl.when(tm <= 1)(cache_two.wait)
@@ -335,7 +338,7 @@
     taps(2, True)
     if N > 2:
         pl.when(tm >= 2)(older)
-    pl.when(tm >= 1)(lambda: forwarded(1, 0))
+    pl.when(jnp.logical_and(tm >= 1, outer))(lambda: forwarded(1, 0))
     from_halo(0)
     taps(0, False)
     pl.when(tm >= 1)(newer)

time: 38.7 us -> 37.1 us (0.959)
  the two profiles are of different devices: /device:TPU:3 before, /device:TPU:11 now
where the time goes in v6:
time: 37.1 us; the launch traced here: 36.9 us
  Pallas kernels  36.2 us (98%)
  local copies, waits for them, and re-layouts  0.73 us (2%)
    pallas_call x1, Pallas kernels, body(): pl.pallas_call(functools.partial(kernel, Z, N), out_shape=jax.ShapeDtypeS...  36.2 us

profile of v6, /device:TPU:11, one launch (start us, length us, event | category | flops | bytes accessed | tf_op | source)
XLA Modules:
  0.0 36.9 jit_solution(6543142387410104965)
XLA Ops:
  0.0 36.2 %shard_map.91 = bf16[1,4,160,192]{3,2,1,0:T(8,128)(2,1)S(1)} custom-call(bf16[1,4,160,192]{3,2,1,0:T(8,128)(2,1)} %x_hbm.1, bf16[2,4,160,384]{3,2,1,0:T(8,128)(2,1)} %cache_hbm.1, bf16[384]{0:T(512)(128)(2,1)} %g1_hbm.1, bf16[384]{0:T(512)(128)(2,1)} %g2_hbm.1, bf16[384,384]{1,0:T(8,128)(2,1)} %wq_hbm.1, bf16[384,384]{1,0:T(8,128)(2,1)} %wk_hbm.1, ...), custom_call_target="tpu_custom_call" | custom-call | tf_op jit(solution)/shard_map/pallas_call | solution.py:414
  36.2 0.7 %copy.11 = bf16[1,4,160,192]{3,2,1,0:T(8,128)(2,1)} copy(bf16[1,4,160,192]{3,2,1,0:T(8,128)(2,1)S(1)} %shard_map.91) | data formatting | bytes 491520
